TPU v7x, 128 devices: a whole 4x4x4 slice. The times are simulated.
128 devices in a mesh: com: 32 (over x, z, y_hi), arc: 4 (over y_lo, core).
Axes of the slice: x: 4, y: 4 (y_hi: 2, y_lo: 2; y = y_hi * 2 + y_lo), z: 4, core: 2. Of those that a mesh axis runs over, the one named last changes fastest.
Arguments:
- lfactor: float32 [64, 768, 768], P('com'), as said below
- links: float32 [64, 768, 4096], P('com', None, 'arc'), may hold values from -0.0546875 to 0.0546875
- usage: int32 [64, 4096], P('com', 'arc'), may hold values 0 or 1
- demands: bfloat16 [64, 768, 256], P('com'), may hold values from -6 to 6
- damping: float32 [4096], P('arc'), may hold values from 0.2 to 1
Outputs:
- schur: float32 [4096, 4096], P('com', 'arc')
- newton_y: float32 [4096, 256], P('arc')
- steps: float32 [64, 768, 256], P('com', None, 'arc')
Inputs may be any that keep to these rules, and one draw needn't show every extreme that they name: lfactor[k] is lower triangular with its diagonal between 1 and 2.
All inputs are finite; a program needn't handle non-finite values. No bound on the sum of `usage` on one device may be relied on, other than what follows from the above.
Results may differ from a plain program's by a relative error of at most 0.003.
Values may be sent and summed in bfloat16 or wider, within the bound.
A program may use at most 192 MiB of HBM per device.

v0:
```python
from functools import partial

import jax
import jax.numpy as jnp
from jax import lax
from jax.sharding import PartitionSpec as P


def on_device(lfactor, links, usage, demands, damping):
    coupling = links * usage[:, None, :].astype(jnp.float32)
    solve_lower = jax.vmap(partial(jax.scipy.linalg.solve_triangular, lower=True))
    transformed = solve_lower(lfactor, coupling).astype(jnp.bfloat16)
    gathered = lax.all_gather(transformed, "arc", axis=2, tiled=True)
    arcs_total = gathered.shape[2]
    tile_width = transformed.shape[2]
    row_count = arcs_total // lax.axis_size("com")
    first_row = lax.axis_index("com") * row_count
    first_column = lax.axis_index("arc") * tile_width
    columns = lax.slice_in_dim(gathered, 0, lax.axis_size("com") * row_count, axis=2)
    schur_block = lax.psum_scatter(
        jnp.einsum("kic,kit->ct", columns, transformed, preferred_element_type=jnp.float32),
        "com",
        scatter_dimension=0,
        tiled=True,
    )
    local_rhs = jnp.einsum("kic,kip->cp", gathered, demands, preferred_element_type=jnp.float32)
    rhs_full = lax.psum(local_rhs, "com")
    rhs_rows = lax.dynamic_slice_in_dim(rhs_full, first_row, row_count, 0)
    rhs_tile = lax.dynamic_slice_in_dim(rhs_full, first_column, tile_width, 0)
    local_product = jnp.dot(schur_block.T, rhs_rows, precision=lax.Precision.HIGHEST)
    product = lax.psum(local_product, "com")
    newton_y = rhs_tile - damping[:, None] * product
    rounded_y = newton_y.astype(jnp.bfloat16)
    partial_terms = jnp.einsum(
        "kit,tp->kip", transformed, rounded_y, preferred_element_type=jnp.float32
    )
    corrections = lax.psum_scatter(
        partial_terms.astype(jnp.bfloat16), "arc", scatter_dimension=2, tiled=True
    ).astype(jnp.float32)
    share_width = corrections.shape[2]
    demand_share = lax.dynamic_slice_in_dim(
        demands, lax.axis_index("arc") * share_width, share_width, 2
    ).astype(jnp.float32)
    solve_upper = jax.vmap(partial(jax.scipy.linalg.solve_triangular, lower=True, trans=1))
    steps = solve_upper(lfactor, demand_share - corrections)
    return (schur_block, newton_y, steps)


def solution(mesh):
    in_specs = (
        P("com", None, None),
        P("com", None, "arc"),
        P("com", "arc"),
        P("com", None, None),
        P("arc"),
    )
    out_specs = (P("com", "arc"), P("arc", None), P("com", None, "arc"))
    return jax.shard_map(
        on_device, mesh=mesh, in_specs=in_specs, out_specs=out_specs, check_vma=False
    )
```

profile of v0, /device:TPU:105, one launch (start us, length us, event | category | flops | bytes accessed | tf_op | source)
XLA Modules:
  0.0 1442.9 jit_solution(490941561665475428)
XLA Ops:
  7.4 4.9 broadcast_select_fusion
  12.4 17.8 %while.1 = (s32[]{:T(128)}, f32[2,768,768]{2,1,0:T(8,128)}, s32[6,2]{0,1:T(2,128)S(1)}, f32[6,2,128,128]{3,2,0,1:T(8,128)S(1)}, s32[]{:T(128)}) while((s32[]{:T(128)}, f32[2,768,768]{2,1,0:T(8,128)}, s32[6,2]{0,1:T(2,128)S(1)}, f32[6,2,128,128]{3,2,0,1:T(8,128)S(1)}, s32[]{:T(128)}) %tuple.29), condition=%wide.while_cond, body=%wide.while_body.sunk | while | flops 2 | bytes 262253 | solution.py:12
  12.4 0.5 fusion.98
  13.0 2.4 bitcast_dynamic-update-slice_fusion.2
  15.4 0.5 fusion.98
  15.9 2.4 bitcast_dynamic-update-slice_fusion.2
  18.4 0.5 fusion.98
  18.9 2.4 bitcast_dynamic-update-slice_fusion.2
  21.4 0.5 fusion.98
  21.9 2.4 bitcast_dynamic-update-slice_fusion.2
  24.4 0.5 fusion.98
  24.9 2.4 bitcast_dynamic-update-slice_fusion.2
  27.3 0.5 fusion.98
  27.8 2.3 bitcast_dynamic-update-slice_fusion.2
  30.2 117.9 %custom-call.7 = f32[2,6,128,128]{2,3,1,0:T(8,128)S(1)} custom-call(f32[2,6,128,128]{3,2,1,0:T(8,128)S(1)} %bitcast.76), custom_call_target="InvertDiagBlocksLowerTriangular" | custom-call | tf_op jit(solution)/shard_map/vmap(jit(_solve_triangular))/triangular_solve | solution.py:12
  148.1 3.5 broadcast_multiply_fusion
  151.6 1.9 convert_dynamic-update-slice_fusion.4
  153.5 1.9 convolution_subtract_fusion.1
  155.6 1.9 convert_dynamic-update-slice_fusion.3
  157.4 2.3 fusion.18
  159.8 1.9 convert_dynamic-update-slice_fusion.2
  161.6 3.1 fusion.21
  164.8 1.9 convert_dynamic-update-slice_fusion.1
  166.7 3.6 fusion.24
  170.4 1.9 convert_dynamic-update-slice_fusion
  172.4 4.3 convolution_subtract_fusion
  176.7 1.9 fusion.27
  178.6 117.0 %all-gather.2.cloned.1.call-done = bf16[2,768,4096]{2,1,0:T(8,128)(2,1)} async-done(((bf16[2,768,1024]{2,1,0:T(8,128)(2,1)}), bf16[2,768,4096]{2,1,0:T(8,128)(2,1)}) %all-gather.2.cloned.1.call-update) | async-done | bytes 12582928 | tf_op jit(solution)/shard_map/all_gather | solution.py:13
  295.6 10.3 convolution_bitcast_fusion.1
  306.0 20.7 %convolution_bitcast_fusion = f32[4096,1024]{1,0:T(8,128)} fusion(bf16[2,768,4096]{2,1,0:T(8,128)(2,1)} %all-gather.2.cloned.1.call-done, bf16[2,768,1024]{2,1,0:T(8,128)(2,1)} %fusion.27), kind=kOutput, calls=%fused_computation.2 | convolution fusion | flops 12884901888 | bytes 32505856 | tf_op jit(solution)/shard_map/kic,kit->ct/dot_general | solution.py:21
  326.8 319.4 %all-reduce.3.cloned.1.call-done = f32[4096,256]{1,0:T(8,128)} async-done(((f32[4096,256]{1,0:T(8,128)}), f32[4096,256]{1,0:T(8,128)}) %all-reduce.3.cloned.1.call-update) | async-done | bytes 4194320 | tf_op jit(solution)/shard_map/psum | solution.py:27
  646.2 391.7 %reduce-scatter.3.cloned.1.call-done = f32[128,1024]{1,0:T(8,128)} async-done(((f32[4096,1024]{1,0:T(8,128)}), f32[128,1024]{1,0:T(8,128)}) %reduce-scatter.3.cloned.1.call-update) | async-done | bytes 524304 | tf_op jit(solution)/shard_map/reduce_scatter | solution.py:20
  1037.8 3.1 fusion.57
  1041.2 329.3 %all-reduce.5.cloned.1.call-done = f32[1024,256]{1,0:T(8,128)} async-done(((f32[1024,256]{1,0:T(8,128)}), f32[1024,256]{1,0:T(8,128)}) %all-reduce.5.cloned.1.call-update) | async-done | bytes 1048592 | tf_op jit(solution)/shard_map/psum | solution.py:31
  1370.5 1.7 multiply_subtract_fusion
  1372.3 4.2 convolution_convert_fusion
  1376.8 48.5 %reduce-scatter.5.cloned.1.call-done = bf16[2,768,64]{1,2,0:T(8,128)(2,1)} async-done(((bf16[2,768,256]{1,2,0:T(8,128)(2,1)}), bf16[2,768,64]{1,2,0:T(8,128)(2,1)}) %reduce-scatter.5.cloned.1.call-update) | async-done | bytes 196624 | tf_op jit(solution)/shard_map/reduce_scatter | solution.py:37
  1425.3 1.0 convert_subtract_fusion
  1426.3 0.4 fusion.67
  1426.6 1.2 convolution_subtract_fusion.4
  1427.8 0.4 fusion.65
  1428.2 1.3 convolution_subtract_fusion.5
  1429.8 1.4 convolution_subtract_fusion.6
  1431.6 1.5 convolution_subtract_fusion.3
  1433.1 0.4 constant_dynamic-update-slice_fusion.9
  1433.5 1.7 convolution_subtract_fusion.2
  1435.2 0.4 convolution_dynamic-update-slice_fusion
  1435.7 0.7 copy-done.2
  (48 shorter events, 2.7 us)
Async XLA Ops:
  7.2 288.5 %copy-start = (bf16[2,768,256]{2,1,0:T(8,128)(2,1)S(1)}, bf16[2,768,256]{2,1,0:T(8,128)(2,1)}, u32[]{:S(2)}) copy-start(bf16[2,768,256]{2,1,0:T(8,128)(2,1)} %param.8) | copy-start | bytes 2359300
  7.2 288.5 %all-gather.2.cloned.1.call-start = ((), (), s32[]{:S(2)}) async-start(), calls=%async_computation.2 | async-start | bytes 15728640 | tf_op jit(solution)/shard_map/all_gather | solution.py:13
  7.4 140.7 %copy-start.3 = (s32[2,1024]{1,0:T(2,128)S(1)}, s32[2,1024]{1,0:T(2,128)}, u32[]{:S(2)}) copy-start(s32[2,1024]{1,0:T(2,128)} %param.7) | copy-start | bytes 24580
  178.6 467.6 %all-reduce.3.cloned.1.call-start = ((), (), s32[]{:S(2)}) async-start(), calls=%async_computation.4 | async-start | bytes 8388608 | tf_op jit(solution)/shard_map/psum | solution.py:27
  305.9 731.9 %reduce-scatter.3.cloned.1.call-start = ((), (), s32[]{:S(2)}) async-start(), calls=%async_computation.3 | async-start | bytes 17301504 | tf_op jit(solution)/shard_map/reduce_scatter | solution.py:20
  326.7 1043.8 %copy-start.4 = (f32[1024]{0:T(1024)S(1)}, f32[1024]{0:T(1024)}, u32[]{:S(2)}) copy-start(f32[1024]{0:T(1024)} %param.9) | copy-start | bytes 12292
  326.7 1043.8 %all-reduce.5.cloned.1.call-start = ((), (), s32[]{:S(2)}) async-start(), calls=%async_computation.5 | async-start | bytes 2097152 | tf_op jit(solution)/shard_map/psum | solution.py:31
  1040.9 384.4 %reduce-scatter.5.cloned.1.call-start = ((), (), s32[]{:S(2)}) async-start(), calls=%async_computation.6 | async-start | bytes 983040 | tf_op jit(solution)/shard_map/reduce_scatter | solution.py:37
  1372.2 57.2 %copy-start.1 = (f32[1024,256]{1,0:T(8,128)}, f32[1024,256]{1,0:T(8,128)S(1)}, u32[]{:S(2)}) copy-start(f32[1024,256]{1,0:T(8,128)S(1)} %multiply_subtract_fusion) | copy-start | bytes 3145732
  1435.6 0.7 copy-start.2
Sparse Core Ops, SparseCore 0:
  178.7 116.8 all-gather.1
  306.1 340.0 all-reduce.2
  649.2 388.6 reduce-scatter.2
  1041.0 329.4 all-reduce.4
  1376.6 48.6 reduce-scatter.4
where the time goes:
time: 1450 us; the launch traced here: 1440 us
  waiting for transfers between devices  1210 us (83%)
  other arithmetic  129 us (9%)
  matrix products  73.8 us (5%)
  local copies, waits for them, and re-layouts  19.3 us (1%)
    reduce_scatter x1, waiting for transfers between devices, on_device(): lax.psum_scatter(jnp.einsum('kic,kit->ct', columns, transformed, preferre...  392 us
    psum x1, waiting for transfers between devices, on_device(): product = lax.psum(local_product, 'com')  329 us
    psum x1, waiting for transfers between devices, on_device(): rhs_full = lax.psum(local_rhs, 'com')  319 us
    another operation x4, other arithmetic, on_device(): transformed = solve_lower(lfactor, coupling).astype(jnp.bfloat16)  123 us
    all_gather x1, waiting for transfers between devices, on_device(): gathered = lax.all_gather(transformed, 'arc', axis=2, tiled=True)  117 us
    reduce_scatter x1, waiting for transfers between devices, on_device(): lax.psum_scatter(partial_terms.astype(jnp.bfloat16), 'arc', scatter_dimen...  48.5 us
  transfers between devices with their start and end apart: 5, of which 5 were waited for; matrix products, arithmetic and copies ran while one was open for 1% of the time, Pallas kernels for 0%

commit v1 on v0

v1 whole, which is shorter than its diff:
```python
import functools
import jax
import jax.numpy as jnp
from jax import lax
from jax.experimental import pallas as pl
from jax.experimental.pallas import tpu as pltpu
from jax.sharding import PartitionSpec as P

F32, BF16 = jnp.float32, jnp.bfloat16
VM = pl.BlockSpec(memory_space=pltpu.VMEM)
ANY = pl.BlockSpec(memory_space=pl.ANY)


def halves(x):
    high = x.astype(BF16)
    return high, (x - high.astype(F32)).astype(BF16)


def mm(a, b):
    return jnp.dot(a, b, preferred_element_type=F32)


def mm3(a, b):
    return mm(a[0], b[0]) + (mm(a[0], b[1]) + mm(a[1], b[0]))


def front_kernel(lf, links, usage, dem, t_out, tt_out, rhs_out, dh, dl, lh, ll, cbuf, mbuf, xbuf, xinv, sems):
    n, nodes, _ = lf.shape
    tiles = nodes // 128
    rows = n * tiles
    copies = [pltpu.make_async_copy(links.at[k], cbuf.at[k], sems.at[k]) for k in range(n)]
    for c in copies:
        c.start()
    lane = lax.broadcasted_iota(jnp.int32, (32, 128), 1)
    for k in range(n):
        for t in range(tiles):
            acc = jnp.zeros((32, 128), F32)
            for p in range(4):
                part = lf[k, t * 128 + 32 * p:t * 128 + 32 * p + 32, t * 128:t * 128 + 128]
                acc = jnp.where(lane // 32 == p, part, acc)
            mbuf[pl.ds((k * tiles + t) * 32, 32), :] = acc
    seg = lax.broadcasted_iota(jnp.int32, (rows, 128), 1)
    for i in range(32):
        a = mbuf[pl.ds(i, rows, stride=32), :]

        def spread(j):
            out = jnp.broadcast_to(a[:, j:j + 1], (rows, 128))
            for p in range(1, 4):
                out = jnp.where(seg // 32 == p, jnp.broadcast_to(a[:, 32 * p + j:32 * p + j + 1], (rows, 128)), out)
            return out

        acc = jnp.where(seg % 32 == i, 1.0, 0.0).astype(F32)
        for j in range(i):
            acc = acc - spread(j) * xbuf[pl.ds(j, rows, stride=32), :]
        xbuf[pl.ds(i, rows, stride=32), :] = acc / spread(i)
    for k in range(n):
        for t in range(tiles):
            part = xbuf[pl.ds((k * tiles + t) * 32, 32), :]
            for p in range(4):
                at = t * 128 + 32 * p
                here = (t % 2) * 128
                xinv[k, at:at + 32, here:here + 128] = jnp.where(lane // 32 == p, part, 0.0)
                xinv[k, at:at + 32, 128 - here:256 - here] = jnp.zeros((32, 128), F32)

    r = lax.broadcasted_iota(jnp.int32, (256, 256), 0)
    c = lax.broadcasted_iota(jnp.int32, (256, 256), 1)

    @pl.loop(0, nodes // 256)
    def _(b):
        at = pl.multiple_of(b * 256, 256)
        block = [lf[k, pl.ds(at, 256), pl.ds(at, 256)] for k in range(n)]
        inv = [xinv[k, pl.ds(at, 256), :] for k in range(n)]
        for s in (32, 64, 128):
            keep = (r // (2 * s) == c // (2 * s)) & (r // s > c // s)
            for k in range(n):
                x = halves(inv[k])
                y = mm3(x, halves(jnp.where(keep, block[k], 0.0)))
                inv[k] = inv[k] - mm3(halves(y), x)
        for k in range(n):
            dh[k, pl.ds(at, 256), :], dl[k, pl.ds(at, 256), :] = halves(inv[k])

    for k in range(n):
        for b in range(1, nodes // 256):
            for e in range(b):
                s = (k, slice(256 * b, 256 * b + 256), slice(256 * e, 256 * e + 256))
                lh[s], ll[s] = halves(lf[s])
        copies[k].wait()

    width = 512
    arcs = cbuf.shape[2]
    blocks = nodes // 256
    for k in range(n):
        @pl.loop(0, arcs // width)
        def _(q):
            cols = pl.ds(pl.multiple_of(q * width, width), width)
            use = usage[pl.ds(k, 1), cols].astype(F32)
            done = []
            for b in range(blocks):
                rest = cbuf[k, 256 * b:256 * b + 256, cols] * use
                for e in range(b):
                    s = (k, slice(256 * b, 256 * b + 256), slice(256 * e, 256 * e + 256))
                    rest = rest - mm3((lh[s], ll[s]), done[e])
                s = (k, slice(256 * b, 256 * b + 256))
                out = mm3((dh[s], dl[s]), halves(rest))
                done.append(halves(out))
                t_out[k * nodes + 256 * b:k * nodes + 256 * b + 256, cols] = done[b][0]
                tt_out[cols, k * nodes + 256 * b:k * nodes + 256 * b + 256] = out.T.astype(BF16)

    @pl.loop(0, arcs // 256)
    def _(q):
        at = pl.ds(pl.multiple_of(q * 256, 256), 256)
        rhs_out[at, :] = mm(tt_out[at, :], dem[...])


def front(lf, links, usage, dem):
    n, nodes, arcs = links.shape
    k = n * nodes
    return pl.pallas_call(
        front_kernel,
        out_shape=(
            jax.ShapeDtypeStruct((k, arcs), BF16),
            jax.ShapeDtypeStruct((arcs, k), BF16),
            jax.ShapeDtypeStruct((arcs, dem.shape[-1]), F32),
            jax.ShapeDtypeStruct((n, nodes, 256), BF16),
            jax.ShapeDtypeStruct((n, nodes, 256), BF16),
            jax.ShapeDtypeStruct((n, nodes, nodes - 256), BF16),
            jax.ShapeDtypeStruct((n, nodes, nodes - 256), BF16),
        ),
        in_specs=[VM, ANY, VM, VM],
        out_specs=[VM] * 7,
        scratch_shapes=[
            pltpu.VMEM((n, nodes, arcs), F32),
            pltpu.VMEM((n * nodes // 4, 128), F32),
            pltpu.VMEM((n * nodes // 4, 128), F32),
            pltpu.VMEM((n, nodes, 256), F32),
            pltpu.SemaphoreType.DMA((n,)),
        ],
        compiler_params=pltpu.CompilerParams(vmem_limit_bytes=60 * 2**20),
        name="front",
    )(lf, links, usage, dem.reshape(k, -1))


MESH = pl.DeviceIdType.MESH


def middle_kernel(t, tt, rp, damp, s_out, y_out, c_out,
                  near, far, cross, sbuf, r1, m1, r2, m2, r3,
                  a1, a2, a3, b1, b2, ag, rhs16,
                  p0, p1, p2, p3, q1, q2, yg,
                  u_send, u_half, u_got, u_all, c_part, c_send, c_near, c_far,
                  tt_s, tt_r, s1x_s, s1x_r, s1z_s, s1z_r, s2_s, s2_r, s3_s, s3_r,
                  ca_s, ca_r, cb_s, cb_r, cc_s, cc_r, w_s, w_r):
    com, arc = lax.axis_index("com"), lax.axis_index("arc")
    x, z, yh = com // 8, (com // 2) % 4, com % 2
    yl, core = arc // 2, arc % 2
    nearby = yl * 2 + 1 - core
    opposite = (1 - yl) * 2 + core
    diagonal = (1 - yl) * 2 + 1 - core

    def at_x(i):
        return (i * 8 + z * 2 + yh, arc)

    def at_z(i):
        return (x * 8 + i * 2 + yh, arc)

    def other(i, o):
        return (i + o) % 4

    partner = (com, nearby)
    facing = (com, opposite)
    mirror = (x * 8 + z * 2 + 1 - yh, arc)

    barrier = pltpu.get_barrier_semaphore()
    for peer in [at_x(other(x, o)) for o in (1, 2, 3)] + [at_z(other(z, o)) for o in (1, 2, 3)] + [partner, facing, mirror]:
        pl.semaphore_signal(barrier, inc=1, device_id=peer, device_id_type=MESH)
    pl.semaphore_wait(barrier, 9)

    def copy(src, dst, send, recv, peer):
        return pltpu.make_async_remote_copy(src_ref=src, dst_ref=dst, send_sem=send, recv_sem=recv, device_id=peer, device_id_type=MESH)

    firsts, seconds = (x, z), (z, x)
    first_at, second_at = (at_x, at_z), (at_z, at_x)
    pending = []

    def go(c):
        c.start()
        pending.append(c)

    def slab(ref, h, i):
        return ref.at[i, :, :, :, pl.ds(0, 128)] if h == 0 else ref.at[:, i, :, :, pl.ds(128, 128)]

    def rs_first(src, dst, sems, which):
        for h in (0, 1):
            for o in (1, 2, 3):
                p = other(firsts[h], o)
                go(copy(slab(src, h, p), dst.at[h, 3 - o], sems[0].at[which, h, o - 1], sems[1].at[which, h, 3 - o], first_at[h](p)))

    def rs_second(src, one, mine, two, sems, which):
        for h in (0, 1):
            for s in range(3):
                copy(one.at[h, s], one.at[h, s], sems[0].at[which, h, s], sems[1].at[which, h, s], partner).wait_recv()
            own = src[firsts[0], :, :, :, 0:128] if h == 0 else src[:, firsts[1], :, :, 128:256]
            total = own.astype(F32)
            for s in range(3):
                total = total + one[h, s].astype(F32)
            mine[h] = total.astype(mine.dtype)
            for o in (1, 2, 3):
                p = other(seconds[h], o)
                go(copy(mine.at[h, p], two.at[h, 3 - o], sems[2].at[which, h, o - 1], sems[3].at[which, h, 3 - o], second_at[h](p)))

    def rs_third(mine, two, mine2, three, sems, which):
        for h in (0, 1):
            for s in range(3):
                copy(two.at[h, s], two.at[h, s], sems[2].at[which, h, s], sems[3].at[which, h, s], partner).wait_recv()
            total = mine[h, seconds[h]].astype(F32)
            for s in range(3):
                total = total + two[h, s].astype(F32)
            mine2[h] = total.astype(mine2.dtype)
            go(copy(mine2.at[h, 1 - yh], three.at[h], sems[4].at[which, h], sems[5].at[which, h], mirror))

    def rs_done(mine2, three, sems, which, h):
        copy(three.at[h], three.at[h], sems[4].at[which, h], sems[5].at[which, h], mirror).wait_recv()
        return mine2[h, yh].astype(F32) + three[h].astype(F32)

    def ag_first(full, sems, which):
        for h in (0, 1):
            here = full.at[h, firsts[h], seconds[h], yh]
            go(copy(here, here, sems[4].at[which, h], sems[5].at[which, h], mirror))

    def ag_second(full, sems, which):
        for h in (0, 1):
            there = full.at[h, firsts[h], seconds[h], 1 - yh]
            copy(there, there, sems[4].at[which, h], sems[5].at[which, h], mirror).wait_recv()
            here = full.at[h, firsts[h], seconds[h]]
            for o in (1, 2, 3):
                go(copy(here, here, sems[2].at[which, h, o - 1], sems[3].at[which, h, 3 - o], second_at[h](other(seconds[h], o))))

    def ag_third(full, sems, which):
        for h in (0, 1):
            for s in range(3):
                there = full.at[h, firsts[h], other(seconds[h], s + 1)]
                copy(there, there, sems[2].at[which, h, s], sems[3].at[which, h, s], partner).wait_recv()
            here = full.at[h, firsts[h]]
            for o in (1, 2, 3):
                go(copy(here, here, sems[0].at[which, h, o - 1], sems[1].at[which, h, 3 - o], first_at[h](other(firsts[h], o))))

    def ag_done(full, sems, which, out):
        for h in (0, 1):
            for s in range(3):
                there = full.at[h, other(firsts[h], s + 1)]
                copy(there, there, sems[0].at[which, h, s], sems[1].at[which, h, s], partner).wait_recv()
        for i in range(4):
            for j in range(4):
                rows = slice((i * 4 + j) * 64, (i * 4 + j) * 64 + 64)
                out[rows, 0:128] = full[0, i, j].reshape(64, 128)
                out[rows, 128:256] = full[1, j, i].reshape(64, 128)

    sems = (ca_s, ca_r, cb_s, cb_r, cc_s, cc_r)

    def piece(q):
        return pl.ds(pl.multiple_of(q * 32, 32), 32)

    def rows_of(source, block, q):
        @pl.loop(0, 4)
        def _(j):
            cols = pl.ds(pl.multiple_of(j * 256, 256), 256)
            left = source[:, piece(q), :].reshape(256, -1)
            sbuf[block, :, :, piece(q), cols] = mm(left, t[:, cols]).astype(BF16).reshape(4, 2, 32, 256)

    def x_copy(block, q):
        slot = (x + 3 - block) % 4
        return copy(sbuf.at[block, :, :, piece(q), pl.ds(0, 512)], r1.at[0, slot, :, :, piece(q)],
                    s1x_s.at[block, q], s1x_r.at[slot, q], at_x(block))

    def z_copy(block, q, o):
        p = other(z, o)
        return copy(sbuf.at[block, p, :, piece(q), pl.ds(512, 512)], r1.at[1, 3 - o, block, :, piece(q)],
                    s1z_s.at[block, q, o - 1], s1z_r.at[3 - o, block, q], at_z(p))

    def send_rows(block, q):
        for o in (1, 2, 3):
            z_copy(block, q, o).start()

        @pl.when(block != x)
        def _():
            x_copy(block, q).start()

    def fold_first(q):
        for s in range(3):
            there = r1.at[0, s, :, :, piece(q)]
            copy(there, there, s1x_s.at[0, q], s1x_r.at[s, q], partner).wait_recv()

        @pl.loop(0, 4)
        def _(i):
            total = sbuf[x, i, :, piece(q), 0:512].astype(F32)
            for s in range(3):
                total = total + r1[0, s, i, :, piece(q)].astype(F32)
            m1[0, i, :, piece(q)] = total.astype(BF16)

        for o in (1, 2, 3):
            second_copy(0, q, o).start()
        for s in range(3):
            for b in range(4):
                there = r1.at[1, s, b, :, piece(q)]
                copy(there, there, s1z_s.at[0, q, s], s1z_r.at[s, b, q], partner).wait_recv()

        @pl.loop(0, 4)
        def _(i):
            total = sbuf[i, z, :, piece(q), 512:1024].astype(F32)
            for s in range(3):
                total = total + r1[1, s, i, :, piece(q)].astype(F32)
            m1[1, i, :, piece(q)] = total.astype(BF16)

        for o in (1, 2, 3):
            second_copy(1, q, o).start()

    def second_copy(h, q, o):
        p = other(seconds[h], o)
        return copy(m1.at[h, p, :, piece(q)], r2.at[h, 3 - o, :, piece(q)], s2_s.at[h, q, o - 1], s2_r.at[h, 3 - o, q], second_at[h](p))

    def own_sum(h, q, k):
        if h == 0:
            total = sbuf[x, z, k, piece(q), 0:512].astype(F32)
        else:
            total = sbuf[x, z, k, piece(q), 512:1024].astype(F32)
        for s in range(3):
            total = total + r1[h, s, seconds[h], k, piece(q)].astype(F32)
        for s in range(3):
            total = total + r2[h, s, k, piece(q)].astype(F32)
        return total

    def third_copy(h, q):
        return copy(m2.at[h, piece(q)], r3.at[h, piece(q)], s3_s.at[h, q], s3_r.at[h, q], mirror)

    def fold_second(q):
        for h in (0, 1):
            for s in range(3):
                there = r2.at[h, s, :, piece(q)]
                copy(there, there, s2_s.at[h, q, s], s2_r.at[h, s, q], partner).wait_recv()
            m2[h, piece(q)] = own_sum(h, q, 1 - yh).astype(BF16)
            third_copy(h, q).start()

    def fold_third(q):
        for h in (0, 1):
            third_copy(h, q).wait_recv()
            s_out[piece(q), 512 * h:512 * h + 512] = own_sum(h, q, yh) + r3[h, piece(q)].astype(F32)

    rs_first(rp, a1, sems, 0)
    go(copy(tt, near, tt_s.at[0], tt_r.at[0], partner))

    def face_copy(q):
        return copy(tt.at[:, piece(q)], far.at[:, piece(q)], tt_s.at[1 + q], tt_r.at[1 + q], facing)

    def forward_copy(q):
        return copy(far.at[:, piece(q)], cross.at[:, piece(q)], tt_s.at[5 + q], tt_r.at[5 + q], partner)

    go(face_copy(0))
    go(face_copy(1))

    def quarter_rows(source, block, low, high):
        @pl.loop(low, high)
        def _(q):
            rows_of(source, block, q)
            send_rows(block, q)

    quarter_rows(tt, arc, 0, 2)
    rs_second(rp, a1, b1, a2, sems, 0)
    quarter_rows(tt, arc, 2, 4)
    rs_third(b1, a2, b2, a3, sems, 0)
    copy(tt, near, tt_s.at[0], tt_r.at[0], partner).wait_recv()
    quarter_rows(near, nearby, 0, 2)
    for h in (0, 1):
        rhs_sum = rs_done(b2, a3, sems, 0, h)
        b2[h, yh] = rhs_sum
        ag[h, firsts[h], seconds[h], yh] = rhs_sum.astype(BF16)
    ag_first(ag, sems, 1)
    quarter_rows(near, nearby, 2, 3)
    ag_second(ag, sems, 1)
    quarter_rows(near, nearby, 3, 4)
    ag_third(ag, sems, 1)
    ag_done(ag, sems, 1, rhs16)

    half = t.shape[0] // 2
    mine_rows = pl.ds(pl.multiple_of(core * half, half), half)
    other_rows = pl.ds(pl.multiple_of((1 - core) * half, half), half)
    u_send[0] = mm(t[other_rows, :], rhs16[...]).astype(BF16)
    go(copy(u_send.at[0], u_got.at[0], w_s.at[0], w_r.at[0], partner))
    u_half[...] = mm(t[mine_rows, :], rhs16[...])
    copy(u_got.at[0], u_got.at[0], w_s.at[0], w_r.at[0], partner).wait_recv()
    u_half[...] += u_got[0].astype(F32)
    u_send[1] = u_half[...].astype(BF16)
    go(copy(u_send.at[1], u_got.at[1], w_s.at[1], w_r.at[1], facing))
    go(face_copy(2))
    go(face_copy(3))

    def far_rows(q):
        face_copy(q).wait_recv()
        go(forward_copy(q))
        rows_of(far, opposite, q)
        send_rows(opposite, q)

    def cross_rows(q):
        forward_copy(q).wait_recv()
        rows_of(cross, diagonal, q)
        send_rows(diagonal, q)

    far_rows(0)
    cross_rows(0)
    far_rows(1)
    copy(u_got.at[1], u_got.at[1], w_s.at[1], w_r.at[1], facing).wait_recv()
    u_all[core] = (u_half[...] + u_got[1].astype(F32)).astype(BF16)
    go(copy(u_all.at[core], u_all.at[core], w_s.at[2], w_r.at[2], partner))
    cross_rows(1)
    there = u_all.at[1 - core]
    copy(there, there, w_s.at[2], w_r.at[2], partner).wait_recv()

    @pl.loop(0, 8)
    def _(j):
        left = tt[j]
        part = mm(left[:, 0:half], u_all[0]) + mm(left[:, half:], u_all[1])
        p0[j // 2, pl.ds(2 * (j % 2), 2)] = part.astype(BF16).reshape(2, 2, 32, 256)

    rs_first(p0, p1, sems, 2)
    fold_first(0)
    rs_second(p0, p1, q1, p2, sems, 2)
    fold_first(1)
    rs_third(q1, p2, q2, p3, sems, 2)
    fold_second(0)
    for h in (0, 1):
        prod = rs_done(q2, p3, sems, 2, h)
        yg[h, firsts[h], seconds[h], yh] = b2[h, yh] - damp[x, z, yh] * prod
    ag_first(yg, sems, 3)
    fold_second(1)
    ag_second(yg, sems, 3)
    far_rows(2)
    ag_third(yg, sems, 3)
    cross_rows(2)
    ag_done(yg, sems, 3, y_out)

    @pl.loop(0, 4)
    def _(j):
        rows = pl.ds(pl.multiple_of(j * 256, 256), 256)
        left = y_out[rows, :].T.astype(BF16)
        right = tt[pl.ds(2 * j, 2)].reshape(256, -1)
        part = mm(left, right)

        @pl.when(j == 0)
        def _():
            c_part[...] = part.reshape(c_part.shape)

        @pl.when(j > 0)
        def _():
            c_part[...] += part.reshape(c_part.shape)

    c_send[0:2] = c_part[:, 1 - core].astype(BF16)
    go(copy(c_send.at[pl.ds(0, 2)], c_near, w_s.at[3], w_r.at[3], partner))
    fold_first(2)
    copy(c_near, c_near, w_s.at[3], w_r.at[3], partner).wait_recv()
    c_send[2] = (c_part[1 - yl, core] + c_near[1 - yl].astype(F32)).astype(BF16)
    go(copy(c_send.at[2], c_far, w_s.at[4], w_r.at[4], facing))
    far_rows(3)
    cross_rows(3)
    fold_second(2)
    fold_third(0)
    fold_third(1)
    fold_first(3)
    fold_third(2)
    copy(c_far, c_far, w_s.at[4], w_r.at[4], facing).wait_recv()
    c_out[...] = c_part[yl, core] + c_near[yl].astype(F32) + c_far[...].astype(F32)
    fold_second(3)
    fold_third(3)

    for c in pending:
        c.wait_send()

    @pl.loop(0, 4)
    def _(q):
        @pl.loop(0, 4)
        def _(block):
            for o in (1, 2, 3):
                z_copy(block, q, o).wait_send()

            @pl.when(block != x)
            def _():
                x_copy(block, q).wait_send()

        for h in (0, 1):
            for o in (1, 2, 3):
                second_copy(h, q, o).wait_send()
            third_copy(h, q).wait_send()


def middle(t, tt, rhs_part, damping):
    rows, arcs = t.shape
    scen = rhs_part.shape[1]
    V, DMA = pltpu.VMEM, pltpu.SemaphoreType.DMA
    tt = tt.reshape(8, 128, rows)
    return pl.pallas_call(
        middle_kernel,
        out_shape=(
            jax.ShapeDtypeStruct((128, arcs), F32),
            jax.ShapeDtypeStruct((arcs, scen), F32),
            jax.ShapeDtypeStruct((64, rows), F32),
        ),
        in_specs=[VM] * 4,
        out_specs=[VM] * 3,
        scratch_shapes=[
            V((8, 128, rows), BF16), V((8, 128, rows), BF16), V((8, 128, rows), BF16),
            V((4, 4, 2, 128, arcs), BF16),
            V((2, 3, 4, 2, 128, 512), BF16), V((2, 4, 2, 128, 512), BF16),
            V((2, 3, 2, 128, 512), BF16), V((2, 128, 512), BF16), V((2, 128, 512), BF16),
            V((2, 3, 4, 2, 32, 128), F32), V((2, 3, 2, 32, 128), F32), V((2, 32, 128), F32),
            V((2, 4, 2, 32, 128), F32), V((2, 2, 32, 128), F32),
            V((2, 4, 4, 2, 32, 128), BF16), V((arcs, scen), BF16),
            V((4, 4, 2, 32, 256), BF16),
            V((2, 3, 4, 2, 32, 128), BF16), V((2, 3, 2, 32, 128), BF16), V((2, 32, 128), BF16),
            V((2, 4, 2, 32, 128), BF16), V((2, 2, 32, 128), BF16),
            V((2, 4, 4, 2, 32, 128), F32),
            V((2, rows // 2, scen), BF16), V((rows // 2, scen), F32), V((2, rows // 2, scen), BF16),
            V((2, rows // 2, scen), BF16),
            V((2, 2, 64, rows), F32), V((3, 64, rows), BF16), V((2, 64, rows), BF16), V((64, rows), BF16),
            DMA((9,)), DMA((9,)),
            DMA((4, 4)), DMA((3, 4)), DMA((4, 4, 3)), DMA((3, 4, 4)),
            DMA((2, 4, 3)), DMA((2, 3, 4)), DMA((2, 4)), DMA((2, 4)),
            DMA((4, 2, 3)), DMA((4, 2, 3)), DMA((4, 2, 3)), DMA((4, 2, 3)), DMA((4, 2)), DMA((4, 2)),
            DMA((5,)), DMA((5,)),
        ],
        compiler_params=pltpu.CompilerParams(
            vmem_limit_bytes=63 * 2**20, collective_id=0, has_side_effects=True
        ),
        name="middle",
    )(t, tt, rhs_part.reshape(4, 4, 2, 32, scen), damping.reshape(4, 4, 2, 32, 1))


def back_kernel(corr, share, dh, dl, lh, ll, out):
    n, nodes, _ = dh.shape
    blocks = nodes // 256
    for k in range(n):
        done = [None] * blocks
        for b in reversed(range(blocks)):
            at = slice(256 * b, 256 * b + 256)
            full = slice(k * nodes + 256 * b, k * nodes + 256 * b + 256)
            rest = share[:, full].astype(F32) - corr[:, full].astype(F32)
            for e in range(b + 1, blocks):
                s = (k, slice(256 * e, 256 * e + 256), at)
                rest = rest - mm3(done[e], (lh[s], ll[s]))
            x = mm3(halves(rest), (dh[k, at, :], dl[k, at, :]))
            done[b] = halves(x)
            out[:, full] = x


def back(corr, share, dh, dl, lh, ll):
    return pl.pallas_call(
        back_kernel,
        out_shape=jax.ShapeDtypeStruct(share.shape, F32),
        in_specs=[VM] * 6,
        out_specs=VM,
        compiler_params=pltpu.CompilerParams(vmem_limit_bytes=60 * 2**20),
        name="back",
    )(corr, share, dh, dl, lh, ll)


def on_device(lfactor, links, usage, demands, damping):
    n, nodes, arcs = links.shape
    scen = demands.shape[2]
    dem = demands.reshape(n * nodes, scen)
    t, tt, rhs_part, dh, dl, lh, ll = front(lfactor, links, usage, dem)
    schur, y, corr = middle(t, tt, rhs_part, damping)
    part = scen // 4
    share = lax.dynamic_slice_in_dim(dem, lax.axis_index("arc") * part, part, 1).T
    steps = back(corr, share, dh, dl, lh, ll)
    return schur, y, steps.reshape(part, n, nodes).transpose(1, 2, 0)


def solution(mesh):
    return jax.shard_map(
        on_device,
        mesh=mesh,
        in_specs=(P("com"), P("com", None, "arc"), P("com", "arc"), P("com"), P("arc")),
        out_specs=(P("com", "arc"), P("arc"), P("com", None, "arc")),
        check_vma=False,
    )
```

time: 1450 us -> 217 us (0.15)
  the two profiles are of different devices: /device:TPU:105 before, /device:TPU:0 now
where the time goes in v1:
time: 217 us
  Pallas kernels  210 us (97%)
  local copies, waits for them, and re-layouts  5.7 us (3%)
    pallas_call x1, Pallas kernels, middle(): pl.pallas_call(middle_kernel, out_shape=(jax.ShapeDtypeStruct((128, arcs)...  175 us
    pallas_call x1, Pallas kernels, front(): pl.pallas_call(front_kernel, out_shape=(jax.ShapeDtypeStruct((k, arcs), B...  29.8 us
    pallas_call x1, Pallas kernels, back(): pl.pallas_call(back_kernel, out_shape=jax.ShapeDtypeStruct(share.shape, F...  5.16 us

profile of v1, /device:TPU:0, one launch (start us, length us, event | category | flops | bytes accessed | tf_op | source)
XLA Modules:
  0.0 216.8 jit_solution(2144558278093564424)
XLA Ops:
  0.6 0.0 copy-start.3
  0.6 29.8 %front.1 = (bf16[1536,1024]{1,0:T(8,128)(2,1)}, bf16[1024,1536]{1,0:T(8,128)(2,1)}, f32[1024,256]{1,0:T(8,128)}, bf16[2,768,256]{2,1,0:T(8,128)(2,1)}, bf16[2,76...) custom-call(f32[2,768,768]{2,1,0:T(8,128)} %lf.1, f32[2,768,1024]{2,1,0:T(8,128)} %links.1, ...), custom_call_target="tpu_custom_call" | custom-call | tf_op jit(solution)/shard_map/front/pallas_call | solution.py:118
  30.5 0.0 copy-done.3
  30.5 1.1 reshape.26.damp
  31.6 0.0 copy-start
  31.6 175.5 %middle.1 = (f32[128,1024]{1,0:T(8,128)}, f32[1024,256]{1,0:T(8,128)}, f32[64,1536]{1,0:T(8,128)}) custom-call(bf16[1536,1024]{1,0:T(8,128)(2,1)} %get-tuple-element.13.t, bf16[8,128,1536]{2,1,0:T(8,128)(2,1)} %bitcast.11, f32[4,4,2,32,256]{4,3,2,1,0:T(8,128)} %bitcast.15, f32[4,4,2,32,1]{4,3,2,1,0:T(8,128)} %reshape.26.damp), custom_call_target="tpu_custom_call" | custom-call | tf_op jit(solution)/shard_map/middle/pallas_call | solution.py:498
  207.1 0.0 copy-done
  207.1 0.2 constant_dynamic-slice_fusion
  207.3 0.8 copy.16
  208.1 0.0 copy-start.2
  208.2 0.0 copy-start.1
  208.2 5.2 %back.1 = f32[64,1536]{1,0:T(8,128)} custom-call(f32[64,1536]{1,0:T(8,128)} %get-tuple-element.18.corr, bf16[64,1536]{1,0:T(8,128)(2,1)} %bitcast.16, bf16[2,768,256]{2,1,0:T(8,128)(2,1)} %get-tuple-element.19.dh, bf16[2,768,256]{2,1,0:T(8,128)(2,1)} %get-tuple-element.20.dl, bf16[2,768,512]{2,1,0:T(8,128)(2,1)} %get-tuple-element.21.lh, ...), custom_call_target="tpu_custom_call" | custom-call | tf_op jit(solution)/shard_map/back/pallas_call | solution.py:553
  213.3 1.8 copy.19
  215.1 0.0 copy-done.2
  215.1 0.8 copy.22
  215.9 0.0 copy-done.1
  215.9 1.0 copy.23
Async XLA Ops:
  0.6 29.8 %copy-start.3 = (f32[1024]{0:T(1024)S(1)}, f32[1024]{0:T(1024)}, u32[]{:S(2)}) copy-start(f32[1024]{0:T(1024)} %param.9) | copy-start | bytes 12292
  31.6 175.5 %copy-start = (bf16[2,768,256]{2,1,0:T(8,128)(2,1)S(1)}, bf16[2,768,256]{2,1,0:T(8,128)(2,1)}, u32[]{:S(2)}) copy-start(bf16[2,768,256]{2,1,0:T(8,128)(2,1)} %param.8) | copy-start | bytes 2359300
  208.1 6.9 %copy-start.2 = (f32[128,1024]{1,0:T(8,128)S(1)}, f32[128,1024]{1,0:T(8,128)}, u32[]{:S(2)}) copy-start(f32[128,1024]{1,0:T(8,128)} %get-tuple-element.26) | copy-start | bytes 1572868
  208.2 7.7 %copy-start.1 = (f32[1024,256]{1,0:T(8,128)S(1)}, f32[1024,256]{1,0:T(8,128)}, u32[]{:S(2)}) copy-start(f32[1024,256]{1,0:T(8,128)} %get-tuple-element.27) | copy-start | bytes 3145732

commit v2 on v1

--- a/solution.py
+++ b/solution.py
@@ -148,7 +148,7 @@
                   a1, a2, a3, b1, b2, ag, rhs16,
                   p0, p1, p2, p3, q1, q2, yg,
                   u_send, u_half, u_got, u_all, c_part, c_send, c_near, c_far,
-                  tt_s, tt_r, s1x_s, s1x_r, s1z_s, s1z_r, s2_s, s2_r, s3_s, s3_r,
+                  xs, xr, x_s, x_r, tt_s, tt_r, s1x_s, s1x_r, s1z_s, s1z_r, s2_s, s2_r, s3_s, s3_r,
                   ca_s, ca_r, cb_s, cb_r, cc_s, cc_r, w_s, w_r):
     com, arc = lax.axis_index("com"), lax.axis_index("arc")
     x, z, yh = com // 8, (com // 2) % 4, com % 2
@@ -173,7 +173,14 @@
     barrier = pltpu.get_barrier_semaphore()
     for peer in [at_x(other(x, o)) for o in (1, 2, 3)] + [at_z(other(z, o)) for o in (1, 2, 3)] + [partner, facing, mirror]:
         pl.semaphore_signal(barrier, inc=1, device_id=peer, device_id_type=MESH)
-    pl.semaphore_wait(barrier, 9)
+    split = x // 2 != yl
+
+    @pl.when(split)
+    def _():
+        for j in range(8):
+            pl.semaphore_signal(barrier, inc=1, device_id=(arc * 8 + j, x), device_id_type=MESH)
+
+    pl.semaphore_wait(barrier, jnp.where(split, 17, 9))
 
     def copy(src, dst, send, recv, peer):
         return pltpu.make_async_remote_copy(src_ref=src, dst_ref=dst, send_sem=send, recv_sem=recv, device_id=peer, device_id_type=MESH)
@@ -252,20 +259,26 @@
         for i in range(4):
             for j in range(4):
                 rows = slice((i * 4 + j) * 64, (i * 4 + j) * 64 + 64)
-                out[rows, 0:128] = full[0, i, j].reshape(64, 128)
-                out[rows, 128:256] = full[1, j, i].reshape(64, 128)
+                out[rows, 0:128] = full[0, i, j].astype(out.dtype).reshape(64, 128)
+                out[rows, 128:256] = full[1, j, i].astype(out.dtype).reshape(64, 128)
 
     sems = (ca_s, ca_r, cb_s, cb_r, cc_s, cc_r)
 
     def piece(q):
         return pl.ds(pl.multiple_of(q * 32, 32), 32)
 
+    half = t.shape[0] // 2
+    given = pl.ds(pl.multiple_of(yl * half, half), half)
+    taken = pl.ds(pl.multiple_of((1 - yl) * half, half), half)
+
     def rows_of(source, block, q):
+        whole = source.shape[2] == 2 * half
+
         @pl.loop(0, 4)
         def _(j):
             cols = pl.ds(pl.multiple_of(j * 256, 256), 256)
             left = source[:, piece(q), :].reshape(256, -1)
-            sbuf[block, :, :, piece(q), cols] = mm(left, t[:, cols]).astype(BF16).reshape(4, 2, 32, 256)
+            sbuf[block, :, :, piece(q), cols] = mm(left, t[:, cols] if whole else t[taken, cols]).astype(BF16).reshape(4, 2, 32, 256)
 
     def x_copy(block, q):
         slot = (x + 3 - block) % 4
@@ -349,38 +362,48 @@
     go(copy(tt, near, tt_s.at[0], tt_r.at[0], partner))
 
     def face_copy(q):
-        return copy(tt.at[:, piece(q)], far.at[:, piece(q)], tt_s.at[1 + q], tt_r.at[1 + q], facing)
+        return copy(tt.at[:, piece(q), given], far.at[:, piece(q)], tt_s.at[1 + q], tt_r.at[1 + q], facing)
 
     def forward_copy(q):
         return copy(far.at[:, piece(q)], cross.at[:, piece(q)], tt_s.at[5 + q], tt_r.at[5 + q], partner)
 
-    go(face_copy(0))
-    go(face_copy(1))
-
-    def quarter_rows(source, block, low, high):
+    def compute_rows(source, block, low, high):
         @pl.loop(low, high)
         def _(q):
             rows_of(source, block, q)
-            send_rows(block, q)
-
-    quarter_rows(tt, arc, 0, 2)
+
+    def far_rows(q):
+        face_copy(q).wait_recv()
+        go(forward_copy(q))
+        rows_of(far, opposite, q)
+
+    def cross_rows(q):
+        forward_copy(q).wait_recv()
+        rows_of(cross, diagonal, q)
+
+    go(face_copy(0))
+    compute_rows(tt, arc, 0, 4)
     rs_second(rp, a1, b1, a2, sems, 0)
-    quarter_rows(tt, arc, 2, 4)
+    copy(tt, near, tt_s.at[0], tt_r.at[0], partner).wait_recv()
+    compute_rows(near, nearby, 0, 2)
     rs_third(b1, a2, b2, a3, sems, 0)
-    copy(tt, near, tt_s.at[0], tt_r.at[0], partner).wait_recv()
-    quarter_rows(near, nearby, 0, 2)
+    send_rows(arc, 0)
+    compute_rows(near, nearby, 2, 3)
     for h in (0, 1):
         rhs_sum = rs_done(b2, a3, sems, 0, h)
         b2[h, yh] = rhs_sum
         ag[h, firsts[h], seconds[h], yh] = rhs_sum.astype(BF16)
     ag_first(ag, sems, 1)
-    quarter_rows(near, nearby, 2, 3)
+    compute_rows(near, nearby, 3, 4)
     ag_second(ag, sems, 1)
-    quarter_rows(near, nearby, 3, 4)
+    go(face_copy(1))
     ag_third(ag, sems, 1)
     ag_done(ag, sems, 1, rhs16)
-
-    half = t.shape[0] // 2
+    send_rows(arc, 1)
+    send_rows(arc, 2)
+    send_rows(nearby, 0)
+    send_rows(nearby, 1)
+
     mine_rows = pl.ds(pl.multiple_of(core * half, half), half)
     other_rows = pl.ds(pl.multiple_of((1 - core) * half, half), half)
     u_send[0] = mm(t[other_rows, :], rhs16[...]).astype(BF16)
@@ -391,26 +414,12 @@
     u_send[1] = u_half[...].astype(BF16)
     go(copy(u_send.at[1], u_got.at[1], w_s.at[1], w_r.at[1], facing))
     go(face_copy(2))
-    go(face_copy(3))
-
-    def far_rows(q):
-        face_copy(q).wait_recv()
-        go(forward_copy(q))
-        rows_of(far, opposite, q)
-        send_rows(opposite, q)
-
-    def cross_rows(q):
-        forward_copy(q).wait_recv()
-        rows_of(cross, diagonal, q)
-        send_rows(diagonal, q)
-
     far_rows(0)
     cross_rows(0)
-    far_rows(1)
     copy(u_got.at[1], u_got.at[1], w_s.at[1], w_r.at[1], facing).wait_recv()
     u_all[core] = (u_half[...] + u_got[1].astype(F32)).astype(BF16)
     go(copy(u_all.at[core], u_all.at[core], w_s.at[2], w_r.at[2], partner))
-    cross_rows(1)
+    far_rows(1)
     there = u_all.at[1 - core]
     copy(there, there, w_s.at[2], w_r.at[2], partner).wait_recv()
 
@@ -421,21 +430,28 @@
         p0[j // 2, pl.ds(2 * (j % 2), 2)] = part.astype(BF16).reshape(2, 2, 32, 256)
 
     rs_first(p0, p1, sems, 2)
-    fold_first(0)
+    cross_rows(1)
     rs_second(p0, p1, q1, p2, sems, 2)
-    fold_first(1)
     rs_third(q1, p2, q2, p3, sems, 2)
-    fold_second(0)
+    send_rows(opposite, 0)
     for h in (0, 1):
         prod = rs_done(q2, p3, sems, 2, h)
-        yg[h, firsts[h], seconds[h], yh] = b2[h, yh] - damp[x, z, yh] * prod
+        yg[h, firsts[h], seconds[h], yh] = (b2[h, yh] - damp[x, z, yh] * prod).astype(BF16)
     ag_first(yg, sems, 3)
-    fold_second(1)
+    send_rows(diagonal, 0)
     ag_second(yg, sems, 3)
+    go(face_copy(3))
     far_rows(2)
     ag_third(yg, sems, 3)
     cross_rows(2)
     ag_done(yg, sems, 3, y_out)
+    send_rows(opposite, 1)
+    send_rows(diagonal, 1)
+    send_rows(arc, 3)
+    send_rows(opposite, 2)
+    send_rows(nearby, 2)
+    send_rows(diagonal, 2)
+    send_rows(nearby, 3)
 
     @pl.loop(0, 4)
     def _(j):
@@ -454,21 +470,42 @@
 
     c_send[0:2] = c_part[:, 1 - core].astype(BF16)
     go(copy(c_send.at[pl.ds(0, 2)], c_near, w_s.at[3], w_r.at[3], partner))
-    fold_first(2)
+    fold_first(0)
+    far_rows(3)
+    send_rows(opposite, 3)
     copy(c_near, c_near, w_s.at[3], w_r.at[3], partner).wait_recv()
     c_send[2] = (c_part[1 - yl, core] + c_near[1 - yl].astype(F32)).astype(BF16)
     go(copy(c_send.at[2], c_far, w_s.at[4], w_r.at[4], facing))
-    far_rows(3)
     cross_rows(3)
-    fold_second(2)
+    send_rows(diagonal, 3)
+    fold_first(1)
+    fold_second(0)
+    fold_first(2)
+    fold_second(1)
+    fold_first(3)
     fold_third(0)
-    fold_third(1)
-    fold_first(3)
-    fold_third(2)
     copy(c_far, c_far, w_s.at[4], w_r.at[4], facing).wait_recv()
     c_out[...] = c_part[yl, core] + c_near[yl].astype(F32) + c_far[...].astype(F32)
+    fold_second(2)
+    fold_third(1)
     fold_second(3)
+    fold_third(2)
     fold_third(3)
+
+    def swap_copy(j, slot):
+        return copy(xs.at[j], xr.at[slot], x_s.at[j], x_r.at[slot], (arc * 8 + j, x))
+
+    @pl.when(split)
+    def _():
+        for j in range(8):
+            xs[j] = s_out[:, 128 * j:128 * j + 128].astype(BF16)
+        for j in range(8):
+            swap_copy(j, z * 2 + yh).start()
+        for j in range(8):
+            swap_copy(j, j).wait_recv()
+            s_out[:, 128 * j:128 * j + 128] += xr[j].astype(F32).T
+        for j in range(8):
+            swap_copy(j, z * 2 + yh).wait_send()
 
     for c in pending:
         c.wait_send()
@@ -505,7 +542,7 @@
         in_specs=[VM] * 4,
         out_specs=[VM] * 3,
         scratch_shapes=[
-            V((8, 128, rows), BF16), V((8, 128, rows), BF16), V((8, 128, rows), BF16),
+            V((8, 128, rows), BF16), V((8, 128, rows // 2), BF16), V((8, 128, rows // 2), BF16),
             V((4, 4, 2, 128, arcs), BF16),
             V((2, 3, 4, 2, 128, 512), BF16), V((2, 4, 2, 128, 512), BF16),
             V((2, 3, 2, 128, 512), BF16), V((2, 128, 512), BF16), V((2, 128, 512), BF16),
@@ -515,10 +552,11 @@
             V((4, 4, 2, 32, 256), BF16),
             V((2, 3, 4, 2, 32, 128), BF16), V((2, 3, 2, 32, 128), BF16), V((2, 32, 128), BF16),
             V((2, 4, 2, 32, 128), BF16), V((2, 2, 32, 128), BF16),
-            V((2, 4, 4, 2, 32, 128), F32),
+            V((2, 4, 4, 2, 32, 128), BF16),
             V((2, rows // 2, scen), BF16), V((rows // 2, scen), F32), V((2, rows // 2, scen), BF16),
             V((2, rows // 2, scen), BF16),
             V((2, 2, 64, rows), F32), V((3, 64, rows), BF16), V((2, 64, rows), BF16), V((64, rows), BF16),
+            V((8, 128, 128), BF16), V((8, 128, 128), BF16), DMA((8,)), DMA((8,)),
             DMA((9,)), DMA((9,)),
             DMA((4, 4)), DMA((3, 4)), DMA((4, 4, 3)), DMA((3, 4, 4)),
             DMA((2, 4, 3)), DMA((2, 3, 4)), DMA((2, 4)), DMA((2, 4)),

time: 217 us -> 199 us (0.917)
  the two profiles are of different devices: /device:TPU:0 before, /device:TPU:105 now
where the time goes in v2:
time: 199 us; the launch traced here: 198 us
  Pallas kernels  192 us (96%)
  local copies, waits for them, and re-layouts  5.7 us (3%)
    pallas_call x1, Pallas kernels, middle(): pl.pallas_call(middle_kernel, out_shape=(jax.ShapeDtypeStruct((128, arcs)...  157 us
    pallas_call x1, Pallas kernels, front(): pl.pallas_call(front_kernel, out_shape=(jax.ShapeDtypeStruct((k, arcs), B...  29.7 us
    pallas_call x1, Pallas kernels, back(): pl.pallas_call(back_kernel, out_shape=jax.ShapeDtypeStruct(share.shape, F...  5.16 us

profile of v2, /device:TPU:105, one launch (start us, length us, event | category | flops | bytes accessed | tf_op | source)
XLA Modules:
  0.0 198.5 jit_solution(13019560373906277101)
XLA Ops:
  0.6 0.0 copy-start.3
  0.6 29.7 %front.1 = (bf16[1536,1024]{1,0:T(8,128)(2,1)}, bf16[1024,1536]{1,0:T(8,128)(2,1)}, f32[1024,256]{1,0:T(8,128)}, bf16[2,768,256]{2,1,0:T(8,128)(2,1)}, bf16[2,76...) custom-call(f32[2,768,768]{2,1,0:T(8,128)} %lf.1, f32[2,768,1024]{2,1,0:T(8,128)} %links.1, ...), custom_call_target="tpu_custom_call" | custom-call | tf_op jit(solution)/shard_map/front/pallas_call | solution.py:118
  30.3 0.0 copy-done.3
  30.3 1.1 reshape.26.damp
  31.5 0.0 copy-start
  31.5 157.3 %middle.1 = (f32[128,1024]{1,0:T(8,128)}, f32[1024,256]{1,0:T(8,128)}, f32[64,1536]{1,0:T(8,128)}) custom-call(bf16[1536,1024]{1,0:T(8,128)(2,1)} %get-tuple-element.13.t, bf16[8,128,1536]{2,1,0:T(8,128)(2,1)} %bitcast.11, f32[4,4,2,32,256]{4,3,2,1,0:T(8,128)} %bitcast.15, f32[4,4,2,32,1]{4,3,2,1,0:T(8,128)} %reshape.26.damp), custom_call_target="tpu_custom_call" | custom-call | tf_op jit(solution)/shard_map/middle/pallas_call | solution.py:535
  188.7 0.0 copy-done
  188.7 0.2 constant_dynamic-slice_fusion
  188.9 0.8 copy.16
  189.8 0.0 copy-start.2
  189.8 0.0 copy-start.1
  189.8 5.2 %back.1 = f32[64,1536]{1,0:T(8,128)} custom-call(f32[64,1536]{1,0:T(8,128)} %get-tuple-element.18.corr, bf16[64,1536]{1,0:T(8,128)(2,1)} %bitcast.16, bf16[2,768,256]{2,1,0:T(8,128)(2,1)} %get-tuple-element.19.dh, bf16[2,768,256]{2,1,0:T(8,128)(2,1)} %get-tuple-element.20.dl, bf16[2,768,512]{2,1,0:T(8,128)(2,1)} %get-tuple-element.21.lh, ...), custom_call_target="tpu_custom_call" | custom-call | tf_op jit(solution)/shard_map/back/pallas_call | solution.py:591
  194.9 1.8 copy.19
  196.7 0.0 copy-done.2
  196.7 0.8 copy.22
  197.5 0.0 copy-done.1
  197.5 1.0 copy.23
Async XLA Ops:
  0.6 29.7 %copy-start.3 = (f32[1024]{0:T(1024)S(1)}, f32[1024]{0:T(1024)}, u32[]{:S(2)}) copy-start(f32[1024]{0:T(1024)} %param.9) | copy-start | bytes 12292
  31.5 157.3 %copy-start = (bf16[2,768,256]{2,1,0:T(8,128)(2,1)S(1)}, bf16[2,768,256]{2,1,0:T(8,128)(2,1)}, u32[]{:S(2)}) copy-start(bf16[2,768,256]{2,1,0:T(8,128)(2,1)} %param.8) | copy-start | bytes 2359300
  189.8 6.9 %copy-start.2 = (f32[128,1024]{1,0:T(8,128)S(1)}, f32[128,1024]{1,0:T(8,128)}, u32[]{:S(2)}) copy-start(f32[128,1024]{1,0:T(8,128)} %get-tuple-element.26) | copy-start | bytes 1572868
  189.8 7.7 %copy-start.1 = (f32[1024,256]{1,0:T(8,128)S(1)}, f32[1024,256]{1,0:T(8,128)}, u32[]{:S(2)}) copy-start(f32[1024,256]{1,0:T(8,128)} %get-tuple-element.27) | copy-start | bytes 3145732

commit v3 on v2

--- a/solution.py
+++ b/solution.py
@@ -24,7 +24,8 @@
     return mm(a[0], b[0]) + (mm(a[0], b[1]) + mm(a[1], b[0]))
 
 
-def front_kernel(lf, links, usage, dem, t_out, tt_out, rhs_out, dh, dl, lh, ll, cbuf, mbuf, xbuf, xinv, sems):
+def front_kernel(lf, links, usage, dem, t_hbm, tt_hbm, rhs_hbm, dh_hbm, dl_hbm, lh_hbm, ll_hbm,
+                 t_out, tt_out, rhs_out, dh, dl, lh, ll, cbuf, mbuf, xbuf, xinv, sems, out_sems):
     n, nodes, _ = lf.shape
     tiles = nodes // 128
     rows = n * tiles
@@ -85,7 +86,14 @@
                 s = (k, slice(256 * b, 256 * b + 256), slice(256 * e, 256 * e + 256))
                 lh[s], ll[s] = halves(lf[s])
         copies[k].wait()
-
+    leaving = []
+
+    def leave(src, dst):
+        leaving.append(pltpu.make_async_copy(src, dst, out_sems.at[len(leaving)]))
+        leaving[-1].start()
+
+    for src, dst in ((dh, dh_hbm), (dl, dl_hbm), (lh, lh_hbm), (ll, ll_hbm)):
+        leave(src, dst)
     width = 512
     arcs = cbuf.shape[2]
     blocks = nodes // 256
@@ -106,18 +114,24 @@
                 t_out[k * nodes + 256 * b:k * nodes + 256 * b + 256, cols] = done[b][0]
                 tt_out[cols, k * nodes + 256 * b:k * nodes + 256 * b + 256] = out.T.astype(BF16)
 
+        mine = pl.ds(k * nodes, nodes)
+        leave(t_out.at[mine], t_hbm.at[mine])
+        leave(tt_out.at[:, mine], tt_hbm.at[:, mine])
+
     @pl.loop(0, arcs // 256)
     def _(q):
         at = pl.ds(pl.multiple_of(q * 256, 256), 256)
         rhs_out[at, :] = mm(tt_out[at, :], dem[...])
 
+    leave(rhs_out, rhs_hbm)
+    for c in leaving:
+        c.wait()
+
 
 def front(lf, links, usage, dem):
     n, nodes, arcs = links.shape
     k = n * nodes
-    return pl.pallas_call(
-        front_kernel,
-        out_shape=(
+    shapes = (
             jax.ShapeDtypeStruct((k, arcs), BF16),
             jax.ShapeDtypeStruct((arcs, k), BF16),
             jax.ShapeDtypeStruct((arcs, dem.shape[-1]), F32),
@@ -125,15 +139,19 @@
             jax.ShapeDtypeStruct((n, nodes, 256), BF16),
             jax.ShapeDtypeStruct((n, nodes, nodes - 256), BF16),
             jax.ShapeDtypeStruct((n, nodes, nodes - 256), BF16),
-        ),
+    )
+    return pl.pallas_call(
+        front_kernel,
+        out_shape=shapes,
         in_specs=[VM, ANY, VM, VM],
-        out_specs=[VM] * 7,
-        scratch_shapes=[
+        out_specs=[ANY] * 7,
+        scratch_shapes=[pltpu.VMEM(a.shape, a.dtype) for a in shapes] + [
             pltpu.VMEM((n, nodes, arcs), F32),
             pltpu.VMEM((n * nodes // 4, 128), F32),
             pltpu.VMEM((n * nodes // 4, 128), F32),
             pltpu.VMEM((n, nodes, 256), F32),
             pltpu.SemaphoreType.DMA((n,)),
+            pltpu.SemaphoreType.DMA((5 + 2 * n,)),
         ],
         compiler_params=pltpu.CompilerParams(vmem_limit_bytes=60 * 2**20),
         name="front",
@@ -143,12 +161,30 @@
 MESH = pl.DeviceIdType.MESH
 
 
-def middle_kernel(t, tt, rp, damp, s_out, y_out, c_out,
-                  near, far, cross, sbuf, r1, m1, r2, m2, r3,
+def upper_solve(corr, share, dh, dl, lh, ll, out):
+    n, nodes, _ = dh.shape
+    blocks = nodes // 256
+    for k in range(n):
+        done = [None] * blocks
+        for b in reversed(range(blocks)):
+            at = slice(256 * b, 256 * b + 256)
+            full = slice(k * nodes + 256 * b, k * nodes + 256 * b + 256)
+            rest = share[:, full].astype(F32) - corr[:, full].astype(F32)
+            for e in range(b + 1, blocks):
+                s = (k, slice(256 * e, 256 * e + 256), at)
+                rest = rest - mm3(done[e], (lh[s], ll[s]))
+            x = mm3(halves(rest), (dh[k, at, :], dl[k, at, :]))
+            done[b] = halves(x)
+            out[k, at, :] = x.T
+
+
+def middle_kernel(damp, t_in, tt_in, rp_in, dem_in, dh_in, dl_in, lh_in, ll_in, s_out, y_out, st_out, c_out,
+                  t, tt, rp, dm, dmt, dh, dl, lh, ll, in_s,
+                  near, far, cross, sbuf, r1, mb, m1, r2, m2, r3,
                   a1, a2, a3, b1, b2, ag, rhs16,
                   p0, p1, p2, p3, q1, q2, yg,
                   u_send, u_half, u_got, u_all, c_part, c_send, c_near, c_far,
-                  xs, xr, x_s, x_r, tt_s, tt_r, s1x_s, s1x_r, s1z_s, s1z_r, s2_s, s2_r, s3_s, s3_r,
+                  xs, xr, x_s, x_r, tt_s, tt_r, s1x_s, s1x_r, s1z_s, s1z_r, sb_s, sb_r, s2_s, s2_r, s3_s, s3_r,
                   ca_s, ca_r, cb_s, cb_r, cc_s, cc_r, w_s, w_r):
     com, arc = lax.axis_index("com"), lax.axis_index("arc")
     x, z, yh = com // 8, (com // 2) % 4, com % 2
@@ -170,6 +206,10 @@
     facing = (com, opposite)
     mirror = (x * 8 + z * 2 + 1 - yh, arc)
 
+    loads = [pltpu.make_async_copy(src, dst, in_s.at[i]) for i, (src, dst) in enumerate(
+        ((rp_in, rp), (tt_in, tt), (t_in, t), (dem_in, dm), (dh_in, dh), (dl_in, dl), (lh_in, lh), (ll_in, ll)))]
+    for c in loads:
+        c.start()
     barrier = pltpu.get_barrier_semaphore()
     for peer in [at_x(other(x, o)) for o in (1, 2, 3)] + [at_z(other(z, o)) for o in (1, 2, 3)] + [partner, facing, mirror]:
         pl.semaphore_signal(barrier, inc=1, device_id=peer, device_id_type=MESH)
@@ -280,52 +320,70 @@
             left = source[:, piece(q), :].reshape(256, -1)
             sbuf[block, :, :, piece(q), cols] = mm(left, t[:, cols] if whole else t[taken, cols]).astype(BF16).reshape(4, 2, 32, 256)
 
-    def x_copy(block, q):
-        slot = (x + 3 - block) % 4
-        return copy(sbuf.at[block, :, :, piece(q), pl.ds(0, 512)], r1.at[0, slot, :, :, piece(q)],
-                    s1x_s.at[block, q], s1x_r.at[slot, q], at_x(block))
-
-    def z_copy(block, q, o):
-        p = other(z, o)
-        return copy(sbuf.at[block, p, :, piece(q), pl.ds(512, 512)], r1.at[1, 3 - o, block, :, piece(q)],
-                    s1z_s.at[block, q, o - 1], s1z_r.at[3 - o, block, q], at_z(p))
+    def flip(i):
+        return i + 1 - 2 * (i % 2)
+
+    def turn(i):
+        return 3 - i
+
+    def ways(q):
+        return (flip, turn) if q % 2 == 0 else (turn, flip)
+
+    def x_copy(q, s):
+        one, two = ways(q)
+        block = one(x) if s == 0 else two(one(x))
+        return block, copy(sbuf.at[block, :, :, piece(q), pl.ds(0, 512)], r1.at[0, s, :, :, piece(q)],
+                           s1x_s.at[s, q], s1x_r.at[s, q], at_x(one(x)))
+
+    def z_copy(block, q, s):
+        one, two = ways(q)
+        part = one(z) if s == 0 else two(one(z))
+        return copy(sbuf.at[block, part, :, piece(q), pl.ds(512, 512)], r1.at[1, s, block, :, piece(q)],
+                    s1z_s.at[s, block, q], s1z_r.at[s, block, q], at_z(one(z)))
+
+    def relay_copy(h, q):
+        two = ways(q)[1]
+        return copy(mb.at[h, :, :, piece(q)], r1.at[h, 2, :, :, piece(q)], sb_s.at[h, q], sb_r.at[h, q], first_at[h](two(firsts[h])))
 
     def send_rows(block, q):
-        for o in (1, 2, 3):
-            z_copy(block, q, o).start()
-
-        @pl.when(block != x)
-        def _():
-            x_copy(block, q).start()
-
-    def fold_first(q):
-        for s in range(3):
-            there = r1.at[0, s, :, :, piece(q)]
-            copy(there, there, s1x_s.at[0, q], s1x_r.at[s, q], partner).wait_recv()
+        for s in (1, 0):
+            z_copy(block, q, s).start()
+            wanted, c = x_copy(q, s)
+            pl.when(block == wanted)(c.start)
+
+    def fold_zero(q):
+        two = ways(q)[1]
+        x_copy(q, 1)[1].wait_recv()
 
         @pl.loop(0, 4)
         def _(i):
-            total = sbuf[x, i, :, piece(q), 0:512].astype(F32)
-            for s in range(3):
-                total = total + r1[0, s, i, :, piece(q)].astype(F32)
-            m1[0, i, :, piece(q)] = total.astype(BF16)
-
-        for o in (1, 2, 3):
-            second_copy(0, q, o).start()
-        for s in range(3):
-            for b in range(4):
-                there = r1.at[1, s, b, :, piece(q)]
-                copy(there, there, s1z_s.at[0, q, s], s1z_r.at[s, b, q], partner).wait_recv()
+            mb[0, i, :, piece(q)] = (sbuf[two(x), i, :, piece(q), 0:512].astype(F32) + r1[0, 1, i, :, piece(q)].astype(F32)).astype(BF16)
+
+        relay_copy(0, q).start()
+        for b in range(4):
+            z_copy(b, q, 1).wait_recv()
 
         @pl.loop(0, 4)
         def _(i):
-            total = sbuf[i, z, :, piece(q), 512:1024].astype(F32)
-            for s in range(3):
-                total = total + r1[1, s, i, :, piece(q)].astype(F32)
-            m1[1, i, :, piece(q)] = total.astype(BF16)
-
-        for o in (1, 2, 3):
-            second_copy(1, q, o).start()
+            mb[1, i, :, piece(q)] = (sbuf[i, two(z), :, piece(q), 512:1024].astype(F32) + r1[1, 1, i, :, piece(q)].astype(F32)).astype(BF16)
+
+        relay_copy(1, q).start()
+
+    def fold_first(q):
+        x_copy(q, 0)[1].wait_recv()
+        for b in range(4):
+            z_copy(b, q, 0).wait_recv()
+        for h in (0, 1):
+            relay_copy(h, q).wait_recv()
+
+            @pl.loop(0, 4)
+            def _(i):
+                own = sbuf[x, i, :, piece(q), 0:512] if h == 0 else sbuf[i, z, :, piece(q), 512:1024]
+                total = own.astype(F32) + r1[h, 0, i, :, piece(q)].astype(F32) + r1[h, 2, i, :, piece(q)].astype(F32)
+                m1[h, i, :, piece(q)] = total.astype(BF16)
+
+            for o in (1, 2, 3):
+                second_copy(h, q, o).start()
 
     def second_copy(h, q, o):
         p = other(seconds[h], o)
@@ -336,7 +394,7 @@
             total = sbuf[x, z, k, piece(q), 0:512].astype(F32)
         else:
             total = sbuf[x, z, k, piece(q), 512:1024].astype(F32)
-        for s in range(3):
+        for s in (0, 2):
             total = total + r1[h, s, seconds[h], k, piece(q)].astype(F32)
         for s in range(3):
             total = total + r2[h, s, k, piece(q)].astype(F32)
@@ -358,7 +416,9 @@
             third_copy(h, q).wait_recv()
             s_out[piece(q), 512 * h:512 * h + 512] = own_sum(h, q, yh) + r3[h, piece(q)].astype(F32)
 
+    loads[0].wait()
     rs_first(rp, a1, sems, 0)
+    loads[1].wait()
     go(copy(tt, near, tt_s.at[0], tt_r.at[0], partner))
 
     def face_copy(q):
@@ -382,6 +442,7 @@
         rows_of(cross, diagonal, q)
 
     go(face_copy(0))
+    loads[2].wait()
     compute_rows(tt, arc, 0, 4)
     rs_second(rp, a1, b1, a2, sems, 0)
     copy(tt, near, tt_s.at[0], tt_r.at[0], partner).wait_recv()
@@ -399,10 +460,11 @@
     go(face_copy(1))
     ag_third(ag, sems, 1)
     ag_done(ag, sems, 1, rhs16)
+    send_rows(nearby, 0)
     send_rows(arc, 1)
+    send_rows(nearby, 1)
     send_rows(arc, 2)
-    send_rows(nearby, 0)
-    send_rows(nearby, 1)
+    send_rows(nearby, 2)
 
     mine_rows = pl.ds(pl.multiple_of(core * half, half), half)
     other_rows = pl.ds(pl.multiple_of((1 - core) * half, half), half)
@@ -416,6 +478,8 @@
     go(face_copy(2))
     far_rows(0)
     cross_rows(0)
+    send_rows(arc, 3)
+    send_rows(nearby, 3)
     copy(u_got.at[1], u_got.at[1], w_s.at[1], w_r.at[1], facing).wait_recv()
     u_all[core] = (u_half[...] + u_got[1].astype(F32)).astype(BF16)
     go(copy(u_all.at[core], u_all.at[core], w_s.at[2], w_r.at[2], partner))
@@ -434,29 +498,27 @@
     rs_second(p0, p1, q1, p2, sems, 2)
     rs_third(q1, p2, q2, p3, sems, 2)
     send_rows(opposite, 0)
+    send_rows(diagonal, 0)
     for h in (0, 1):
         prod = rs_done(q2, p3, sems, 2, h)
         yg[h, firsts[h], seconds[h], yh] = (b2[h, yh] - damp[x, z, yh] * prod).astype(BF16)
     ag_first(yg, sems, 3)
-    send_rows(diagonal, 0)
+    send_rows(opposite, 1)
     ag_second(yg, sems, 3)
     go(face_copy(3))
     far_rows(2)
     ag_third(yg, sems, 3)
+    send_rows(diagonal, 1)
     cross_rows(2)
+    fold_zero(0)
     ag_done(yg, sems, 3, y_out)
-    send_rows(opposite, 1)
-    send_rows(diagonal, 1)
-    send_rows(arc, 3)
     send_rows(opposite, 2)
-    send_rows(nearby, 2)
     send_rows(diagonal, 2)
-    send_rows(nearby, 3)
 
     @pl.loop(0, 4)
     def _(j):
         rows = pl.ds(pl.multiple_of(j * 256, 256), 256)
-        left = y_out[rows, :].T.astype(BF16)
+        left = y_out[rows, :].astype(F32).T.astype(BF16)
         right = tt[pl.ds(2 * j, 2)].reshape(256, -1)
         part = mm(left, right)
 
@@ -470,6 +532,7 @@
 
     c_send[0:2] = c_part[:, 1 - core].astype(BF16)
     go(copy(c_send.at[pl.ds(0, 2)], c_near, w_s.at[3], w_r.at[3], partner))
+    fold_zero(1)
     fold_first(0)
     far_rows(3)
     send_rows(opposite, 3)
@@ -479,15 +542,22 @@
     cross_rows(3)
     send_rows(diagonal, 3)
     fold_first(1)
+    fold_zero(2)
     fold_second(0)
+    fold_zero(3)
+    fold_second(1)
     fold_first(2)
-    fold_second(1)
+    fold_third(0)
     fold_first(3)
-    fold_third(0)
+    fold_third(1)
     copy(c_far, c_far, w_s.at[4], w_r.at[4], facing).wait_recv()
     c_out[...] = c_part[yl, core] + c_near[yl].astype(F32) + c_far[...].astype(F32)
+    for c in loads[3:]:
+        c.wait()
+    for b in range(6):
+        dmt[:, 256 * b:256 * b + 256] = dm[256 * b:256 * b + 256, :].astype(F32).T
+    upper_solve(c_out, dmt.at[pl.ds(pl.multiple_of(arc * 64, 64), 64)], dh, dl, lh, ll, st_out)
     fold_second(2)
-    fold_third(1)
     fold_second(3)
     fold_third(2)
     fold_third(3)
@@ -510,24 +580,20 @@
     for c in pending:
         c.wait_send()
 
-    @pl.loop(0, 4)
-    def _(q):
-        @pl.loop(0, 4)
-        def _(block):
-            for o in (1, 2, 3):
-                z_copy(block, q, o).wait_send()
-
-            @pl.when(block != x)
-            def _():
-                x_copy(block, q).wait_send()
-
+    for q in range(4):
+        for s in (0, 1):
+            for block in range(4):
+                z_copy(block, q, s).wait_send()
+            x_copy(q, s)[1].wait_send()
+        for h in (0, 1):
+            relay_copy(h, q).wait_send()
         for h in (0, 1):
             for o in (1, 2, 3):
                 second_copy(h, q, o).wait_send()
             third_copy(h, q).wait_send()
 
 
-def middle(t, tt, rhs_part, damping):
+def middle(t, tt, rhs_part, damping, dem, dh, dl, lh, ll):
     rows, arcs = t.shape
     scen = rhs_part.shape[1]
     V, DMA = pltpu.VMEM, pltpu.SemaphoreType.DMA
@@ -536,15 +602,17 @@
         middle_kernel,
         out_shape=(
             jax.ShapeDtypeStruct((128, arcs), F32),
-            jax.ShapeDtypeStruct((arcs, scen), F32),
-            jax.ShapeDtypeStruct((64, rows), F32),
+            jax.ShapeDtypeStruct((arcs, scen), BF16),
+            jax.ShapeDtypeStruct((dh.shape[0], dh.shape[1], 64), F32),
         ),
-        in_specs=[VM] * 4,
+        in_specs=[VM] + [ANY] * 8,
         out_specs=[VM] * 3,
         scratch_shapes=[
+            V((64, rows), F32), V((rows, arcs), BF16), V((8, 128, rows), BF16), V((4, 4, 2, 32, scen), F32),
+            V((rows, scen), BF16), V((scen, rows), F32), V(dh.shape, BF16), V(dl.shape, BF16), V(lh.shape, BF16), V(ll.shape, BF16), DMA((8,)),
             V((8, 128, rows), BF16), V((8, 128, rows // 2), BF16), V((8, 128, rows // 2), BF16),
             V((4, 4, 2, 128, arcs), BF16),
-            V((2, 3, 4, 2, 128, 512), BF16), V((2, 4, 2, 128, 512), BF16),
+            V((2, 3, 4, 2, 128, 512), BF16), V((2, 4, 2, 128, 512), BF16), V((2, 4, 2, 128, 512), BF16),
             V((2, 3, 2, 128, 512), BF16), V((2, 128, 512), BF16), V((2, 128, 512), BF16),
             V((2, 3, 4, 2, 32, 128), F32), V((2, 3, 2, 32, 128), F32), V((2, 32, 128), F32),
             V((2, 4, 2, 32, 128), F32), V((2, 2, 32, 128), F32),
@@ -558,7 +626,7 @@
             V((2, 2, 64, rows), F32), V((3, 64, rows), BF16), V((2, 64, rows), BF16), V((64, rows), BF16),
             V((8, 128, 128), BF16), V((8, 128, 128), BF16), DMA((8,)), DMA((8,)),
             DMA((9,)), DMA((9,)),
-            DMA((4, 4)), DMA((3, 4)), DMA((4, 4, 3)), DMA((3, 4, 4)),
+            DMA((2, 4)), DMA((2, 4)), DMA((2, 4, 4)), DMA((2, 4, 4)), DMA((2, 4)), DMA((2, 4)),
             DMA((2, 4, 3)), DMA((2, 3, 4)), DMA((2, 4)), DMA((2, 4)),
             DMA((4, 2, 3)), DMA((4, 2, 3)), DMA((4, 2, 3)), DMA((4, 2, 3)), DMA((4, 2)), DMA((4, 2)),
             DMA((5,)), DMA((5,)),
@@ -567,47 +635,15 @@
             vmem_limit_bytes=63 * 2**20, collective_id=0, has_side_effects=True
         ),
         name="middle",
-    )(t, tt, rhs_part.reshape(4, 4, 2, 32, scen), damping.reshape(4, 4, 2, 32, 1))
-
-
-def back_kernel(corr, share, dh, dl, lh, ll, out):
-    n, nodes, _ = dh.shape
-    blocks = nodes // 256
-    for k in range(n):
-        done = [None] * blocks
-        for b in reversed(range(blocks)):
-            at = slice(256 * b, 256 * b + 256)
-            full = slice(k * nodes + 256 * b, k * nodes + 256 * b + 256)
-            rest = share[:, full].astype(F32) - corr[:, full].astype(F32)
-            for e in range(b + 1, blocks):
-                s = (k, slice(256 * e, 256 * e + 256), at)
-                rest = rest - mm3(done[e], (lh[s], ll[s]))
-            x = mm3(halves(rest), (dh[k, at, :], dl[k, at, :]))
-            done[b] = halves(x)
-            out[:, full] = x
-
-
-def back(corr, share, dh, dl, lh, ll):
-    return pl.pallas_call(
-        back_kernel,
-        out_shape=jax.ShapeDtypeStruct(share.shape, F32),
-        in_specs=[VM] * 6,
-        out_specs=VM,
-        compiler_params=pltpu.CompilerParams(vmem_limit_bytes=60 * 2**20),
-        name="back",
-    )(corr, share, dh, dl, lh, ll)
+    )(damping.reshape(4, 4, 2, 32, 1), t, tt, rhs_part.reshape(4, 4, 2, 32, scen), dem, dh, dl, lh, ll)
 
 
 def on_device(lfactor, links, usage, demands, damping):
     n, nodes, arcs = links.shape
-    scen = demands.shape[2]
-    dem = demands.reshape(n * nodes, scen)
+    dem = demands.reshape(n * nodes, demands.shape[2])
     t, tt, rhs_part, dh, dl, lh, ll = front(lfactor, links, usage, dem)
-    schur, y, corr = middle(t, tt, rhs_part, damping)
-    part = scen // 4
-    share = lax.dynamic_slice_in_dim(dem, lax.axis_index("arc") * part, part, 1).T
-    steps = back(corr, share, dh, dl, lh, ll)
-    return schur, y, steps.reshape(part, n, nodes).transpose(1, 2, 0)
+    schur, y, steps = middle(t, tt, rhs_part, damping, dem, dh, dl, lh, ll)
+    return schur, y.astype(F32), steps
 
 
 def solution(mesh):

time: 199 us -> 175 us (0.88)
  Pallas kernels: 192 us -> 166 us
  other arithmetic: 0 us -> 2.09 us
    pallas_call x1, Pallas kernels: 157 us -> 139 us  [middle(): pl.pallas_call(middle_kernel, out_shape=(jax.ShapeDtypeStruct((128, arcs)...]
    pallas_call x2 -> x1, Pallas kernels: 34.8 us -> 26.7 us  [front(): pl.pallas_call(front_kernel, out_shape=shapes, in_specs=[VM, ANY, VM, VM]...]
    convert_element_type x0 -> x1, other arithmetic: none -> 2.09 us  [on_device(): return (schur, y.astype(F32), steps)]
    unnamed x11 -> x2, local copies, waits for them, and re-layouts: 2.62 us -> 4.01 us
where the time goes in v3:
time: 175 us; the launch traced here: 174 us
  Pallas kernels  166 us (95%)
  local copies, waits for them, and re-layouts  5.83 us (3%)
  other arithmetic  2.09 us (1%)
    pallas_call x1, Pallas kernels, middle(): pl.pallas_call(middle_kernel, out_shape=(jax.ShapeDtypeStruct((128, arcs)...  139 us
    pallas_call x1, Pallas kernels, front(): pl.pallas_call(front_kernel, out_shape=shapes, in_specs=[VM, ANY, VM, VM]...  26.7 us
    unnamed x2, local copies, waits for them, and re-layouts  4.01 us

profile of v3, /device:TPU:105, one launch (start us, length us, event | category | flops | bytes accessed | tf_op | source)
XLA Modules:
  0.0 174.4 jit_solution(8281793073125884017)
XLA Ops:
  0.6 1.8 %reshape.22.damp = f32[4,4,2,32,1]{4,3,2,1,0:T(8,128)} reshape(f32[1024]{0:T(1024)} %param.9) | data formatting | bytes 8192 | tf_op jit(solution)/shard_map/reshape | solution.py:638
  2.4 26.7 %front.1 = (bf16[1536,1024]{1,0:T(8,128)(2,1)}, bf16[1024,1536]{1,0:T(8,128)(2,1)}, f32[1024,256]{1,0:T(8,128)}, bf16[2,768,256]{2,1,0:T(8,128)(2,1)}, bf16[2,76...) custom-call(f32[2,768,768]{2,1,0:T(8,128)} %lf.1, f32[2,768,1024]{2,1,0:T(8,128)} %links.1, ...), custom_call_target="tpu_custom_call" | custom-call | tf_op jit(solution)/shard_map/front/pallas_call | solution.py:143
  29.1 139.2 %middle.1 = (f32[128,1024]{1,0:T(8,128)}, bf16[1024,256]{1,0:T(8,128)(2,1)}, f32[2,768,64]{2,1,0:T(8,128)}) custom-call(f32[4,4,2,32,1]{4,3,2,1,0:T(8,128)} %reshape.22.damp, bf16[1536,1024]{1,0:T(8,128)(2,1)} %get-tuple-element.13.t_in, bf16[8,128,1536]{2,1,0:T(8,128)(2,1)} %bitcast.5, f32[4,4,2,32,256]{4,3,2,1,0:T(8,128)} %bitcast.6, ...), custom_call_target="tpu_custom_call" | custom-call | tf_op jit(solution)/shard_map/middle/pallas_call | solution.py:601
  168.3 2.1 %copy.10 = f32[2,768,64]{1,2,0:T(8,128)} copy(f32[2,768,64]{2,1,0:T(8,128)} %get-tuple-element.28) | data formatting | bytes 786432
  170.4 2.1 %convert_element_type.3 = f32[1024,256]{1,0:T(8,128)} convert(bf16[1024,256]{1,0:T(8,128)(2,1)} %get-tuple-element.21) | non-fusion elementwise | flops 262144 | bytes 1572864 | tf_op jit(solution)/shard_map/convert_element_type | solution.py:646
  172.5 1.9 %copy.12 = f32[128,1024]{1,0:T(8,128)} copy(f32[128,1024]{1,0:T(8,128)} %get-tuple-element.32) | data formatting | bytes 1048576

commit v4 on v3

--- a/solution.py
+++ b/solution.py
@@ -175,7 +175,7 @@
                 rest = rest - mm3(done[e], (lh[s], ll[s]))
             x = mm3(halves(rest), (dh[k, at, :], dl[k, at, :]))
             done[b] = halves(x)
-            out[k, at, :] = x.T
+            out[k, :, at] = x
 
 
 def middle_kernel(damp, t_in, tt_in, rp_in, dem_in, dh_in, dl_in, lh_in, ll_in, s_out, y_out, st_out, c_out,
@@ -449,6 +449,7 @@
     compute_rows(near, nearby, 0, 2)
     rs_third(b1, a2, b2, a3, sems, 0)
     send_rows(arc, 0)
+    send_rows(nearby, 0)
     compute_rows(near, nearby, 2, 3)
     for h in (0, 1):
         rhs_sum = rs_done(b2, a3, sems, 0, h)
@@ -460,7 +461,6 @@
     go(face_copy(1))
     ag_third(ag, sems, 1)
     ag_done(ag, sems, 1, rhs16)
-    send_rows(nearby, 0)
     send_rows(arc, 1)
     send_rows(nearby, 1)
     send_rows(arc, 2)
@@ -499,18 +499,22 @@
     rs_third(q1, p2, q2, p3, sems, 2)
     send_rows(opposite, 0)
     send_rows(diagonal, 0)
+    lanes = lax.broadcasted_iota(jnp.int32, (32, 128), 1)
+    place = lax.broadcasted_iota(jnp.int32, (32, 128), 0) + (com % 4) * 32
+    scale = jnp.sum(jnp.where(lanes == place, damp[pl.ds(com // 4, 1), :], 0.0), axis=1, keepdims=True)
     for h in (0, 1):
         prod = rs_done(q2, p3, sems, 2, h)
-        yg[h, firsts[h], seconds[h], yh] = (b2[h, yh] - damp[x, z, yh] * prod).astype(BF16)
+        yg[h, firsts[h], seconds[h], yh] = (b2[h, yh] - scale * prod).astype(BF16)
     ag_first(yg, sems, 3)
     send_rows(opposite, 1)
     ag_second(yg, sems, 3)
     go(face_copy(3))
+    fold_zero(0)
     far_rows(2)
     ag_third(yg, sems, 3)
     send_rows(diagonal, 1)
     cross_rows(2)
-    fold_zero(0)
+    fold_first(0)
     ag_done(yg, sems, 3, y_out)
     send_rows(opposite, 2)
     send_rows(diagonal, 2)
@@ -533,7 +537,6 @@
     c_send[0:2] = c_part[:, 1 - core].astype(BF16)
     go(copy(c_send.at[pl.ds(0, 2)], c_near, w_s.at[3], w_r.at[3], partner))
     fold_zero(1)
-    fold_first(0)
     far_rows(3)
     send_rows(opposite, 3)
     copy(c_near, c_near, w_s.at[3], w_r.at[3], partner).wait_recv()
@@ -603,7 +606,7 @@
         out_shape=(
             jax.ShapeDtypeStruct((128, arcs), F32),
             jax.ShapeDtypeStruct((arcs, scen), BF16),
-            jax.ShapeDtypeStruct((dh.shape[0], dh.shape[1], 64), F32),
+            jax.ShapeDtypeStruct((dh.shape[0], 64, dh.shape[1]), F32),
         ),
         in_specs=[VM] + [ANY] * 8,
         out_specs=[VM] * 3,
@@ -635,15 +638,31 @@
             vmem_limit_bytes=63 * 2**20, collective_id=0, has_side_effects=True
         ),
         name="middle",
-    )(damping.reshape(4, 4, 2, 32, 1), t, tt, rhs_part.reshape(4, 4, 2, 32, scen), dem, dh, dl, lh, ll)
+    )(damping.reshape(8, 128), t, tt, rhs_part.reshape(4, 4, 2, 32, scen), dem, dh, dl, lh, ll)
+
+
+def write_kernel(schur, y, steps, schur_out, y_out, steps_out):
+    schur_out[...] = schur[...]
+    y_out[...] = y[...].astype(F32)
+    steps_out[...] = steps[...]
+
+
+def write(*arrays):
+    return pl.pallas_call(
+        write_kernel,
+        out_shape=tuple(jax.ShapeDtypeStruct(a.shape, F32) for a in arrays),
+        in_specs=[VM] * 3,
+        out_specs=[VM] * 3,
+        name="write",
+    )(*arrays)
 
 
 def on_device(lfactor, links, usage, demands, damping):
     n, nodes, arcs = links.shape
     dem = demands.reshape(n * nodes, demands.shape[2])
     t, tt, rhs_part, dh, dl, lh, ll = front(lfactor, links, usage, dem)
-    schur, y, steps = middle(t, tt, rhs_part, damping, dem, dh, dl, lh, ll)
-    return schur, y.astype(F32), steps
+    schur, y, steps = write(*middle(t, tt, rhs_part, damping, dem, dh, dl, lh, ll))
+    return schur, y, steps.transpose(0, 2, 1)
 
 
 def solution(mesh):

time: 175 us -> 168 us (0.960)
  local copies, waits for them, and re-layouts: 5.83 us -> 0 us
  other arithmetic: 2.09 us -> 0 us
  Pallas kernels: 166 us -> 168 us
    unnamed x2 -> x0, local copies, waits for them, and re-layouts: 4.01 us -> none
    pallas_call x0 -> x1, Pallas kernels: none -> 2.66 us  [write(): pl.pallas_call(write_kernel, out_shape=tuple((jax.ShapeDtypeStruct(a.shap...]
    convert_element_type x1 -> x0, other arithmetic: 2.09 us -> none  [on_device(): return (schur, y.astype(F32), steps)]
    reshape x1 -> x0, local copies, waits for them, and re-layouts: 1.82 us -> none  [middle(): damping.reshape(4, 4, 2, 32, 1)]
where the time goes in v4:
time: 168 us
  Pallas kernels  168 us (100%)
    pallas_call x1, Pallas kernels, middle(): pl.pallas_call(middle_kernel, out_shape=(jax.ShapeDtypeStruct((128, arcs)...  138 us
    pallas_call x1, Pallas kernels, front(): pl.pallas_call(front_kernel, out_shape=shapes, in_specs=[VM, ANY, VM, VM]...  26.7 us

profile of v4, /device:TPU:105, one launch (start us, length us, event | category | flops | bytes accessed | tf_op | source)
XLA Modules:
  0.0 168.2 jit_solution(14932299549472153344)
XLA Ops:
  0.6 26.7 %front.1 = (bf16[1536,1024]{1,0:T(8,128)(2,1)}, bf16[1024,1536]{1,0:T(8,128)(2,1)}, f32[1024,256]{1,0:T(8,128)}, bf16[2,768,256]{2,1,0:T(8,128)(2,1)}, bf16[2,76...) custom-call(f32[2,768,768]{2,1,0:T(8,128)} %lf.1, f32[2,768,1024]{2,1,0:T(8,128)} %links.1, ...), custom_call_target="tpu_custom_call" | custom-call | tf_op jit(solution)/shard_map/front/pallas_call | solution.py:143
  27.3 138.2 %middle.1 = (f32[128,1024]{1,0:T(8,128)}, bf16[1024,256]{1,0:T(8,128)(2,1)}, f32[2,64,768]{2,1,0:T(8,128)}) custom-call(f32[8,128]{1,0:T(8,128)} %bitcast.9, bf16[1536,1024]{1,0:T(8,128)(2,1)} %get-tuple-element.16.t_in, bf16[8,128,1536]{2,1,0:T(8,128)(2,1)} %bitcast.7, f32[4,4,2,32,256]{4,3,2,1,0:T(8,128)} %bitcast.8, bf16[1536,256]{1,0:T(8,128)(2,1)} %bitcast.6, ...), custom_call_target="tpu_custom_call" | custom-call | tf_op jit(solution)/shard_map/middle/pallas_call | solution.py:604
  165.6 2.7 %write.1 = (f32[128,1024]{1,0:T(8,128)}, f32[1024,256]{1,0:T(8,128)}, f32[2,64,768]{2,1,0:T(8,128)}) custom-call(f32[128,1024]{1,0:T(8,128)} %get-tuple-element.23.schur, bf16[1024,256]{1,0:T(8,128)(2,1)} %get-tuple-element.24.y, f32[2,64,768]{2,1,0:T(8,128)} %get-tuple-element.25.steps), custom_call_target="tpu_custom_call" | custom-call | tf_op jit(solution)/shard_map/write/pallas_call | solution.py:651
